TPU v7x, 32 devices: a whole 2x2x4 slice. The times are simulated.
32 devices in a mesh: clus: 8 (over z, core), lvl: 4 (over y, x).
Axes of the slice: x: 2, y: 2, z: 4, core: 2. Of those that a mesh axis runs over, the one named last changes fastest.
Arguments:
- krylov_basis: float32 [8, 4, 2048], P(None, 'lvl', 'clus'), may hold values from -90 to 90
- near_block: bfloat16 [4, 8, 4, 256, 256], P('lvl', 'clus'), may hold values from -1 to 2.5
- near_col: int32 [4, 8, 4], P('lvl', 'clus'), may hold values from 0 to 7, as said below
- near_count: int32 [4, 8], P('lvl', 'clus'), may hold values from 1 to 4, as said below
- far_col: int32 [4, 8, 6], P('lvl', 'clus'), may hold values from 0 to 7, as said below
- v_basis: bfloat16 [4, 8, 32, 256], P('lvl', 'clus'), may hold values from -0.375 to 0.375
- u_basis: bfloat16 [4, 8, 32, 256], P('lvl', 'clus'), may hold values from -1 to 1
- far_coupling: float32 [4, 8, 6, 32, 32], P('lvl', 'clus'), may hold values from -0.4375 to 0.4375
- transfer: float32 [4, 8, 32, 32], P('lvl', 'clus'), may hold values from -1 to 1
- top_coupling: float32 [4, 8, 4, 32, 32], P('lvl', 'clus'), may hold values from -0.5 to 0.5
Outputs:
- q_next: float32 [4, 4, 2048], P(None, 'lvl', 'clus')
- coeffs: float32 [2, 12, 4], replicated
Inputs may be any that keep to these rules, and one draw needn't show every extreme that they name: `near_col`: slot 0 of every leaf names the leaf itself; every other slot names leaf i - 1 or leaf i + 1 of the same subtree. Slots at or beyond the leaf's near_count name such leaves too, and their blocks are ignored. `near_count`: in some aligned run of 1 leaves every leaf has 4. `far_col`: A partner lies in the same subtree, in an aligned run of 1 leaves other than the leaf's own. Slot 0 names a leaf of the run just before the leaf's own, runs counted cyclically within the subtree.
All inputs are finite; a program needn't handle non-finite values.
Results may differ from a plain program's by a relative error of at most 0.00037.
Values may be sent and summed in bfloat16 or wider, within the bound.
No kernel may reach another device: no remote copies, remote signals or barrier semaphores. Data moves between devices by JAX's collectives and lax.ppermute only.
A program may use at most 64 MiB of HBM per device.

v0:
```python
import jax
import jax.numpy as jnp
from jax import lax
from jax.sharding import PartitionSpec as P

LEAF = 256
RANK = 32
VECS = 4
NEAR_SLOTS = 4
FAR_SLOTS = 6
STEPS = 2
LEAVES_DEV = 1
BASIS = 8
PRECISE = lax.Precision.HIGHEST


def padded_2(block, sides, width):
    for axis, dim in sides:
        count = lax.axis_size(axis)
        forward = [(i, i + 1) for i in range(count - 1)]
        backward = [(target, source) for source, target in forward]
        low = lax.ppermute(
            lax.slice_in_dim(block, block.shape[dim] - width, None, axis=dim), axis, forward
        )
        high = lax.ppermute(lax.slice_in_dim(block, 0, width, axis=dim), axis, backward)
        block = jnp.concatenate([low, block, high], axis=dim)
    return block


def row_products(left_rows, right_rows):
    return jnp.dot(left_rows, right_rows.T, precision=PRECISE)


def near_field(lowered, near_block, near_col, near_count):
    padded = padded_2(lowered, (("clus", 1),), LEAVES_DEV * LEAF)
    leaf_rows = padded.reshape(VECS, 3 * LEAVES_DEV, LEAF)
    first_leaf = (lax.axis_index("clus") - 1) * LEAVES_DEV
    partner_cols = jnp.clip(near_col[0] - first_leaf, 0, 3 * LEAVES_DEV - 1)
    live_count = near_count[0]
    blocks = near_block[0]
    picked = jnp.take(leaf_rows, partner_cols.reshape(-1), axis=1).reshape(
        VECS, LEAVES_DEV, NEAR_SLOTS, LEAF
    )
    slot_ids = lax.broadcasted_iota(jnp.int32, (LEAVES_DEV, NEAR_SLOTS), 1)
    is_live = slot_ids < live_count[:, None]
    picked = jnp.where(is_live[None, :, :, None], picked, jnp.zeros_like(picked))
    result = jnp.einsum("lkpq,vlkq->vlp", blocks, picked, preferred_element_type=jnp.float32)
    return result


def far_field(lowered, far_col, v_basis, u_basis, far_coupling, transfer, top_coupling):
    leaves = lowered.reshape(VECS, LEAVES_DEV, LEAF)
    skeleton = jnp.einsum("lrp,vlp->lvr", v_basis[0], leaves, preferred_element_type=jnp.float32)
    flat_skel = skeleton.reshape(LEAVES_DEV, VECS * RANK)
    wanted = far_col[0].reshape(-1)
    arrived = lax.all_gather(flat_skel, "clus", axis=0, tiled=True)
    arrived_rows = arrived.shape[0]
    matches = (wanted[:, None] == lax.broadcasted_iota(jnp.int32, (1, arrived_rows), 1)).astype(
        jnp.float32
    )
    partners = jnp.dot(matches, arrived, precision=PRECISE)
    partners = partners.reshape(LEAVES_DEV, FAR_SLOTS, VECS, RANK)
    coupled = jnp.einsum("lkqr,lkvr->lvq", far_coupling[0], partners, precision=PRECISE)
    coarse = jnp.einsum("lvr,lrq->vq", skeleton, transfer[0], precision=PRECISE)
    everyone = lax.all_gather(coarse.reshape(1, VECS * RANK), "lvl", axis=0, tiled=True)
    everyone = everyone.reshape(-1, VECS, RANK)
    own_tree = lax.axis_index("lvl")
    couplings = top_coupling[0, 0]
    others = lax.broadcasted_iota(jnp.int32, (couplings.shape[0], 1, 1), 0) != own_tree
    couplings = jnp.where(others, couplings, jnp.zeros_like(couplings))
    upper = jnp.einsum("tqr,tvr->vq", couplings, everyone, precision=PRECISE)
    coupled = coupled + jnp.einsum("lqr,vr->lvq", transfer[0], upper, precision=PRECISE)
    coupled_low = coupled.astype(jnp.bfloat16)
    return jnp.einsum("lvq,lqp->vlp", coupled_low, u_basis[0], preferred_element_type=jnp.float32)


def orthogonalize(window, image_block):
    rows_all = float(lax.axis_size("clus") * lax.axis_size("lvl") * image_block.shape[1])
    metric, projection, square = lax.psum(
        (
            row_products(window, window),
            row_products(window, image_block),
            row_products(image_block, image_block),
        ),
        ("clus", "lvl"),
    )
    metric = metric / rows_all
    projection = projection / rows_all
    square = square / rows_all
    remainder = image_block - jnp.dot(projection.T, window, precision=PRECISE)
    coef_cross = jnp.dot(projection.T, projection, precision=PRECISE)
    weighted = jnp.dot(
        projection.T, jnp.dot(metric, projection, precision=PRECISE), precision=PRECISE
    )
    gram = square - 2.0 * coef_cross + weighted
    lower_factor = jnp.linalg.cholesky(gram)
    inverse = lax.linalg.triangular_solve(
        lower_factor, jnp.eye(VECS, dtype=jnp.float32), left_side=True, lower=True
    )
    new_block = jnp.dot(inverse, remainder, precision=PRECISE)
    return (new_block, jnp.concatenate([projection, lower_factor.T], axis=0))


def local(
    krylov_basis,
    near_block,
    near_col,
    near_count,
    far_col,
    v_basis,
    u_basis,
    far_coupling,
    transfer,
    top_coupling,
):
    row_count = krylov_basis.shape[2]
    window = krylov_basis.reshape(BASIS, row_count)
    current = window[VECS:]
    records = []
    for step_index in range(STEPS):
        lowered = current.astype(jnp.bfloat16)
        near_part = near_field(lowered, near_block, near_col, near_count)
        far_part = far_field(
            lowered, far_col, v_basis, u_basis, far_coupling, transfer, top_coupling
        )
        image_block = (near_part + far_part).reshape(VECS, row_count)
        current, record = orthogonalize(window, image_block)
        records.append(record)
        window = jnp.concatenate([window[VECS:], current], axis=0)
    return (current.reshape(VECS, 1, row_count), jnp.stack(records))


def solution(mesh):
    return jax.shard_map(
        local,
        mesh=mesh,
        in_specs=(
            P(None, "lvl", "clus"),
            P("lvl", "clus", None, None, None),
            P("lvl", "clus", None),
            P("lvl", "clus"),
            P("lvl", "clus", None),
            P("lvl", "clus", None, None),
            P("lvl", "clus", None, None),
            P("lvl", "clus", None, None, None),
            P("lvl", "clus", None, None),
            P("lvl", "clus", None, None, None),
        ),
        out_specs=(P(None, "lvl", "clus"), P()),
        check_vma=False,
    )
```

profile of v0, /device:TPU:10, one launch (start us, length us, event | category | flops | bytes accessed | tf_op | source)
XLA Modules:
  0.0 142.5 jit_solution(8753681522929081642)
XLA Ops:
  0.7 0.7 slice.13
  1.4 2.0 %collective-permute-start.1 = (bf16[4,256]{1,0:T(4,128)(2,1)S(1)}, bf16[4,256]{1,0:T(4,128)(2,1)S(1)}, u32[]{:S(2)}, u32[]{:S(2)}) collective-permute-start(bf16[4,256]{1,0:T(4,128)(2,1)S(1)} %bitcast.165), channel_id=1, source_target_pairs={{4,0},{8,4},{12,8},{16,12},{20,16},{24,20},{28,24},{5,1},{9,5},{13... | collective-permute-start | bytes 6152 | tf_op jit(solution)/shard_map/ppermute | solution.py:25
  3.5 2.4 %collective-permute-start = (bf16[4,256]{1,0:T(4,128)(2,1)S(1)}, bf16[4,256]{1,0:T(4,128)(2,1)S(1)}, u32[]{:S(2)}, u32[]{:S(2)}) collective-permute-start(bf16[4,256]{1,0:T(4,128)(2,1)S(1)} %bitcast.166), channel_id=1, source_target_pairs={{0,4},{4,8},{8,12},{12,16},{16,20},{20,24},{24,28},{1,5},{5,9},{9,... | collective-permute-start | bytes 6152 | tf_op jit(solution)/shard_map/ppermute | solution.py:22
  6.9 9.1 %all-gather = f32[8,1,128]{2,1,0:T(1,128)S(1)} all-gather(f32[1,1,128]{2,1,0:T(1,128)S(1)} %reshape.212), channel_id=1, replica_groups=mesh['clus'=8,'lvl'=4] {'clus'}, dimensions={0}, use_global_device_ids=true | all-gather | bytes 4608 | tf_op jit(solution)/shard_map/all_gather | solution.py:56
  16.2 0.6 copy-done.3
  17.1 8.0 %all-gather.1 = f32[4,1,128]{2,1,0:T(1,128)S(1)} all-gather(f32[1,1,128]{2,1,0:T(1,128)S(1)} %reshape.214), channel_id=1, replica_groups=mesh['clus'=8,'lvl'=4] {'lvl'}, dimensions={0}, use_global_device_ids=true | all-gather | bytes 2560 | tf_op jit(solution)/shard_map/all_gather | solution.py:65
  25.1 0.5 broadcast.208
  25.6 0.7 reduce.10
  26.5 0.3 convolution_bitcast_fusion.8
  27.0 0.6 gather_fusion
  27.6 0.2 convolution_bitcast_fusion.4
  27.9 0.5 copy-done.6
  28.7 41.9 %all-reduce.1 = (f32[4,4]{0,1:T(4,128)S(1)}, f32[8,4]{0,1:T(4,128)S(1)}, f32[8,8]{1,0:T(8,128)S(1)}) all-reduce(f32[4,4]{0,1:T(4,128)S(1)} %fusion.88, f32[8,4]{0,1:T(4,128)S(1)} %convolution_bitcast_fusion.7, f32[8,8]{1,0:T(8,128)S(1)} %fusion.29), channel_id=1, replica_groups=mesh['clus'=8,'lvl'=4] {'clus','lvl'}, use_global_device_ids=true, to_apply=%region_0.2 | all-reduce | flops 112 | bytes 896 | tf_op jit(solution)/shard_map/psum | solution.py:79
  71.2 0.4 cholesky.44
  71.6 0.6 compare_reduce_fusion.1
  72.3 0.6 fusion.74
  72.9 0.3 custom-call.6
  73.6 1.9 %collective-permute-start.3 = (bf16[4,256]{1,0:T(4,128)(2,1)S(1)}, bf16[4,256]{1,0:T(4,128)(2,1)S(1)}, u32[]{:S(2)}, u32[]{:S(2)}) collective-permute-start(bf16[4,256]{1,0:T(4,128)(2,1)S(1)} %get-tuple-element.23), channel_id=1, source_target_pairs={{4,0},{8,4},{12,8},{16,12},{20,16},{24,20},{28,24},{5,1},{9,5},{13... | collective-permute-start | bytes 6152 | tf_op jit(solution)/shard_map/ppermute | solution.py:25
  75.5 2.4 %collective-permute-start.2 = (bf16[4,256]{1,0:T(4,128)(2,1)S(1)}, bf16[4,256]{1,0:T(4,128)(2,1)S(1)}, u32[]{:S(2)}, u32[]{:S(2)}) collective-permute-start(bf16[4,256]{1,0:T(4,128)(2,1)S(1)} %get-tuple-element.23), channel_id=1, source_target_pairs={{0,4},{4,8},{8,12},{12,16},{16,20},{20,24},{24,28},{1,5},{5,9},{9,... | collective-permute-start | bytes 6152 | tf_op jit(solution)/shard_map/ppermute | solution.py:22
  78.3 8.1 %all-gather.2 = f32[8,1,128]{2,1,0:T(1,128)S(1)} all-gather(f32[1,1,128]{2,1,0:T(1,128)S(1)} %reshape.216), channel_id=1, replica_groups=mesh['clus'=8,'lvl'=4] {'clus'}, dimensions={0}, use_global_device_ids=true | all-gather | bytes 4608 | tf_op jit(solution)/shard_map/all_gather | solution.py:56
  86.9 8.0 %all-gather.3 = f32[4,1,128]{2,1,0:T(1,128)S(1)} all-gather(f32[1,1,128]{2,1,0:T(1,128)S(1)} %reshape.218), channel_id=1, replica_groups=mesh['clus'=8,'lvl'=4] {'lvl'}, dimensions={0}, use_global_device_ids=true | all-gather | bytes 2560 | tf_op jit(solution)/shard_map/all_gather | solution.py:65
  94.9 0.7 reduce.11
  95.6 0.2 convolution_bitcast_fusion.5
  96.2 0.6 gather_fusion.1
  96.8 0.2 convolution_bitcast_fusion.3
  97.4 40.8 %all-reduce = (f32[4,4]{0,1:T(4,128)S(1)}, f32[8,4]{0,1:T(4,128)S(1)}, f32[8,8]{1,0:T(8,128)S(1)}) all-reduce(f32[4,4]{0,1:T(4,128)S(1)} %fusion.89, f32[8,4]{0,1:T(4,128)S(1)} %fusion.42, f32[8,8]{1,0:T(8,128)S(1)} %fusion.41), channel_id=1, replica_groups=mesh['clus'=8,'lvl'=4] {'clus','lvl'}, use_global_device_ids=true, to_apply=%region_5.9 | all-reduce | flops 112 | bytes 896 | tf_op jit(solution)/shard_map/psum | solution.py:79
  138.9 0.4 cholesky.55
  139.3 0.6 compare_reduce_fusion
  139.9 0.6 fusion.73
  140.6 0.3 custom-call.7
  141.2 0.6 copy.47
  141.9 0.6 pad_maximum_fusion.6
  (75 shorter events, 5.5 us)
Async XLA Ops:
  0.6 27.0 %copy-start = (bf16[1,1,4,256,256]{4,3,2,1,0:T(8,128)(2,1)S(1)}, bf16[1,1,4,256,256]{4,3,2,1,0:T(8,128)(2,1)}, u32[]{:S(2)}) copy-start(bf16[1,1,4,256,256]{4,3,2,1,0:T(8,128)(2,1)} %param.16) | copy-start | bytes 1572868
  0.6 5.3 %copy-start.4 = (f32[8,1,256]{2,1,0:T(1,128)S(1)}, f32[8,1,256]{2,1,0:T(1,128)}, u32[]{:S(2)}) copy-start(f32[8,1,256]{2,1,0:T(1,128)} %param.15) | copy-start | bytes 24580
  0.7 5.4 %copy-start.7 = (s32[1,1,4]{2,1,0:T(1,128)S(1)}, s32[1,1,4]{2,1,0:T(1,128)}, u32[]{:S(2)}) copy-start(s32[1,1,4]{2,1,0:T(1,128)} %param.17) | copy-start | bytes 52
  0.7 6.1 %copy-start.5 = (bf16[1,1,32,256]{3,2,1,0:T(8,128)(2,1)S(1)}, bf16[1,1,32,256]{3,2,1,0:T(8,128)(2,1)}, u32[]{:S(2)}) copy-start(bf16[1,1,32,256]{3,2,1,0:T(8,128)(2,1)} %param.20) | copy-start | bytes 49156
  0.7 15.3 %copy-start.8 = (s32[1,1,6]{2,1,0:T(1,128)S(1)}, s32[1,1,6]{2,1,0:T(1,128)}, u32[]{:S(2)}) copy-start(s32[1,1,6]{2,1,0:T(1,128)} %param.19) | copy-start | bytes 76
  1.4 24.9 %copy-start.1 = (f32[1,1,6,32,32]{4,3,2,1,0:T(8,128)S(1)}, f32[1,1,6,32,32]{4,3,2,1,0:T(8,128)}, u32[]{:S(2)}) copy-start(f32[1,1,6,32,32]{4,3,2,1,0:T(8,128)} %param.22) | copy-start | bytes 73732
  1.4 25.5 %collective-permute-start.1 = (bf16[4,256]{1,0:T(4,128)(2,1)S(1)}, bf16[4,256]{1,0:T(4,128)(2,1)S(1)}, u32[]{:S(2)}, u32[]{:S(2)}) collective-permute-start(bf16[4,256]{1,0:T(4,128)(2,1)S(1)} %bitcast.165), channel_id=1, source_target_pairs={{4,0},{8,4},{12,8},{16,12},{20,16},{24,20},{28,24},{5,1},{9,5},{13... | collective-permute-start | bytes 6152 | tf_op jit(solution)/shard_map/ppermute | solution.py:25
  3.5 23.5 %collective-permute-start = (bf16[4,256]{1,0:T(4,128)(2,1)S(1)}, bf16[4,256]{1,0:T(4,128)(2,1)S(1)}, u32[]{:S(2)}, u32[]{:S(2)}) collective-permute-start(bf16[4,256]{1,0:T(4,128)(2,1)S(1)} %bitcast.166), channel_id=1, source_target_pairs={{0,4},{4,8},{8,12},{12,16},{16,20},{20,24},{24,28},{1,5},{5,9},{9,... | collective-permute-start | bytes 6152 | tf_op jit(solution)/shard_map/ppermute | solution.py:22
  16.2 0.7 copy-start.3
  25.6 1.0 copy-start.2
  27.6 0.7 copy-start.6
  73.6 22.6 %collective-permute-start.3 = (bf16[4,256]{1,0:T(4,128)(2,1)S(1)}, bf16[4,256]{1,0:T(4,128)(2,1)S(1)}, u32[]{:S(2)}, u32[]{:S(2)}) collective-permute-start(bf16[4,256]{1,0:T(4,128)(2,1)S(1)} %get-tuple-element.23), channel_id=1, source_target_pairs={{4,0},{8,4},{12,8},{16,12},{20,16},{24,20},{28,24},{5,1},{9,5},{13... | collective-permute-start | bytes 6152 | tf_op jit(solution)/shard_map/ppermute | solution.py:25
  75.5 20.7 %collective-permute-start.2 = (bf16[4,256]{1,0:T(4,128)(2,1)S(1)}, bf16[4,256]{1,0:T(4,128)(2,1)S(1)}, u32[]{:S(2)}, u32[]{:S(2)}) collective-permute-start(bf16[4,256]{1,0:T(4,128)(2,1)S(1)} %get-tuple-element.23), channel_id=1, source_target_pairs={{0,4},{4,8},{8,12},{12,16},{16,20},{20,24},{24,28},{1,5},{5,9},{9,... | collective-permute-start | bytes 6152 | tf_op jit(solution)/shard_map/ppermute | solution.py:22
where the time goes:
time: 143 us
  blocking collectives  116 us (81%)
  starting transfers between devices  8.78 us (6%)
  other arithmetic  6.2 us (4%)
  matrix products  5.25 us (4%)
  local copies, waits for them, and re-layouts  5.02 us (4%)
  between operations  1.52 us (1%)
    psum x2, blocking collectives, orthogonalize(): lax.psum((row_products(window, window), row_products(window, image_block)...  82.6 us
    all_gather x2, blocking collectives, far_field(): arrived = lax.all_gather(flat_skel, 'clus', axis=0, tiled=True)  17.2 us
    all_gather x2, blocking collectives, far_field(): lax.all_gather(coarse.reshape(1, VECS * RANK), 'lvl', axis=0, tiled=True)  15.9 us
    ppermute x2, starting transfers between devices, padded_2(): lax.ppermute(lax.slice_in_dim(block, block.shape[dim] - width, None, axis...  4.81 us
    ppermute x2, starting transfers between devices, padded_2(): lax.ppermute(lax.slice_in_dim(block, 0, width, axis=dim), axis, backward)  3.96 us
  transfers between devices with their start and end apart: 4, of which 0 were waited for; matrix products, arithmetic and copies ran while one was open for 3% of the time, Pallas kernels for 0%

commit v1 on v0

--- a/solution.py
+++ b/solution.py
@@ -77,12 +77,15 @@
 def orthogonalize(window, image_block):
     rows_all = float(lax.axis_size("clus") * lax.axis_size("lvl") * image_block.shape[1])
     metric, projection, square = lax.psum(
-        (
-            row_products(window, window),
-            row_products(window, image_block),
-            row_products(image_block, image_block),
+        lax.psum(
+            (
+                row_products(window, window),
+                row_products(window, image_block),
+                row_products(image_block, image_block),
+            ),
+            "lvl",
         ),
-        ("clus", "lvl"),
+        "clus",
     )
     metric = metric / rows_all
     projection = projection / rows_all

time: 143 us -> 112 us (0.78)
  the two profiles are of different devices: /device:TPU:10 before, /device:TPU:0 now
where the time goes in v1:
time: 112 us
  blocking collectives  84.7 us (76%)
  starting transfers between devices  8.77 us (8%)
  other arithmetic  6.2 us (6%)
  matrix products  5.25 us (5%)
  local copies, waits for them, and re-layouts  5.02 us (4%)
  between operations  1.55 us (1%)
    psum x2, blocking collectives, orthogonalize(): lax.psum(lax.psum((row_products(window, window), row_products(window, ima...  27.8 us
    all_gather x2, blocking collectives, far_field(): arrived = lax.all_gather(flat_skel, 'clus', axis=0, tiled=True)  22.8 us
    psum x2, blocking collectives, orthogonalize(): lax.psum((row_products(window, window), row_products(window, image_block)...  18.2 us
    all_gather x2, blocking collectives, far_field(): lax.all_gather(coarse.reshape(1, VECS * RANK), 'lvl', axis=0, tiled=True)  15.9 us
    ppermute x2, starting transfers between devices, padded_2(): lax.ppermute(lax.slice_in_dim(block, block.shape[dim] - width, None, axis...  6.06 us
    ppermute x2, starting transfers between devices, padded_2(): lax.ppermute(lax.slice_in_dim(block, 0, width, axis=dim), axis, backward)  2.71 us
  transfers between devices with their start and end apart: 4, of which 0 were waited for; matrix products, arithmetic and copies ran while one was open for 4% of the time, Pallas kernels for 0%

profile of v1, /device:TPU:0, one launch (start us, length us, event | category | flops | bytes accessed | tf_op | source)
XLA Modules:
  0.0 111.5 jit_solution(11979445094377019396)
XLA Ops:
  0.7 0.7 slice.13
  1.4 1.4 %collective-permute-start.1 = (bf16[4,256]{1,0:T(4,128)(2,1)S(1)}, bf16[4,256]{1,0:T(4,128)(2,1)S(1)}, u32[]{:S(2)}, u32[]{:S(2)}) collective-permute-start(bf16[4,256]{1,0:T(4,128)(2,1)S(1)} %bitcast.165), channel_id=1, source_target_pairs={{4,0},{8,4},{12,8},{16,12},{20,16},{24,20},{28,24},{5,1},{9,5},{13... | collective-permute-start | bytes 6152 | tf_op jit(solution)/shard_map/ppermute | solution.py:25
  2.9 3.0 %collective-permute-start = (bf16[4,256]{1,0:T(4,128)(2,1)S(1)}, bf16[4,256]{1,0:T(4,128)(2,1)S(1)}, u32[]{:S(2)}, u32[]{:S(2)}) collective-permute-start(bf16[4,256]{1,0:T(4,128)(2,1)S(1)} %bitcast.166), channel_id=1, source_target_pairs={{0,4},{4,8},{8,12},{12,16},{16,20},{20,24},{24,28},{1,5},{5,9},{9,... | collective-permute-start | bytes 6152 | tf_op jit(solution)/shard_map/ppermute | solution.py:22
  6.9 13.5 %all-gather = f32[8,1,128]{2,1,0:T(1,128)S(1)} all-gather(f32[1,1,128]{2,1,0:T(1,128)S(1)} %reshape.212), channel_id=1, replica_groups=mesh['clus'=8,'lvl'=4] {'clus'}, dimensions={0}, use_global_device_ids=true | all-gather | bytes 4608 | tf_op jit(solution)/shard_map/all_gather | solution.py:56
  20.6 0.6 copy-done.3
  21.5 8.0 %all-gather.1 = f32[4,1,128]{2,1,0:T(1,128)S(1)} all-gather(f32[1,1,128]{2,1,0:T(1,128)S(1)} %reshape.214), channel_id=1, replica_groups=mesh['clus'=8,'lvl'=4] {'lvl'}, dimensions={0}, use_global_device_ids=true | all-gather | bytes 2560 | tf_op jit(solution)/shard_map/all_gather | solution.py:65
  29.5 0.5 broadcast.208
  30.0 0.7 reduce.10
  30.9 0.3 convolution_bitcast_fusion.8
  31.4 0.6 gather_fusion
  32.0 0.2 convolution_bitcast_fusion.4
  32.3 0.5 copy-done.6
  33.1 9.1 %all-reduce.3 = (f32[4,4]{0,1:T(4,128)S(1)}, f32[8,4]{0,1:T(4,128)S(1)}, f32[8,8]{1,0:T(8,128)S(1)}) all-reduce(f32[4,4]{0,1:T(4,128)S(1)} %fusion.88, f32[8,4]{0,1:T(4,128)S(1)} %convolution_bitcast_fusion.7, f32[8,8]{1,0:T(8,128)S(1)} %fusion.29), channel_id=1, replica_groups=mesh['clus'=8,'lvl'=4] {'lvl'}, use_global_device_ids=true, to_apply=%region_0.2 | all-reduce | flops 112 | bytes 896 | tf_op jit(solution)/shard_map/psum | solution.py:80
  42.2 13.9 %all-reduce.1 = (f32[4,4]{0,1:T(4,128)S(1)}, f32[8,4]{0,1:T(4,128)S(1)}, f32[8,8]{1,0:T(8,128)S(1)}) all-reduce(f32[4,4]{0,1:T(4,128)S(1)} %get-tuple-element.20, f32[8,4]{0,1:T(4,128)S(1)} %get-tuple-element.21, f32[8,8]{1,0:T(8,128)S(1)} %get-tuple-element.22), channel_id=1, replica_groups=mesh['clus'=8,'lvl'=4] {'clus'}, use_global_device_ids=true, to_apply=%region_1.3 | all-reduce | flops 112 | bytes 896 | tf_op jit(solution)/shard_map/psum | solution.py:79
  56.8 0.4 cholesky.44
  57.2 0.6 compare_reduce_fusion.1
  57.8 0.6 fusion.74
  58.5 0.3 custom-call.6
  59.2 1.3 %collective-permute-start.3 = (bf16[4,256]{1,0:T(4,128)(2,1)S(1)}, bf16[4,256]{1,0:T(4,128)(2,1)S(1)}, u32[]{:S(2)}, u32[]{:S(2)}) collective-permute-start(bf16[4,256]{1,0:T(4,128)(2,1)S(1)} %get-tuple-element.29), channel_id=1, source_target_pairs={{4,0},{8,4},{12,8},{16,12},{20,16},{24,20},{28,24},{5,1},{9,5},{13... | collective-permute-start | bytes 6152 | tf_op jit(solution)/shard_map/ppermute | solution.py:25
  60.5 3.0 %collective-permute-start.2 = (bf16[4,256]{1,0:T(4,128)(2,1)S(1)}, bf16[4,256]{1,0:T(4,128)(2,1)S(1)}, u32[]{:S(2)}, u32[]{:S(2)}) collective-permute-start(bf16[4,256]{1,0:T(4,128)(2,1)S(1)} %get-tuple-element.29), channel_id=1, source_target_pairs={{0,4},{4,8},{8,12},{12,16},{16,20},{20,24},{24,28},{1,5},{5,9},{9,... | collective-permute-start | bytes 6152 | tf_op jit(solution)/shard_map/ppermute | solution.py:22
  63.8 9.4 %all-gather.2 = f32[8,1,128]{2,1,0:T(1,128)S(1)} all-gather(f32[1,1,128]{2,1,0:T(1,128)S(1)} %reshape.216), channel_id=1, replica_groups=mesh['clus'=8,'lvl'=4] {'clus'}, dimensions={0}, use_global_device_ids=true | all-gather | bytes 4608 | tf_op jit(solution)/shard_map/all_gather | solution.py:56
  73.7 7.9 %all-gather.3 = f32[4,1,128]{2,1,0:T(1,128)S(1)} all-gather(f32[1,1,128]{2,1,0:T(1,128)S(1)} %reshape.218), channel_id=1, replica_groups=mesh['clus'=8,'lvl'=4] {'lvl'}, dimensions={0}, use_global_device_ids=true | all-gather | bytes 2560 | tf_op jit(solution)/shard_map/all_gather | solution.py:65
  81.6 0.7 reduce.11
  83.0 0.6 gather_fusion.1
  84.2 9.1 %all-reduce.2 = (f32[4,4]{0,1:T(4,128)S(1)}, f32[8,4]{0,1:T(4,128)S(1)}, f32[8,8]{1,0:T(8,128)S(1)}) all-reduce(f32[4,4]{0,1:T(4,128)S(1)} %fusion.89, f32[8,4]{0,1:T(4,128)S(1)} %fusion.42, f32[8,8]{1,0:T(8,128)S(1)} %fusion.41), channel_id=1, replica_groups=mesh['clus'=8,'lvl'=4] {'lvl'}, use_global_device_ids=true, to_apply=%region_8.12 | all-reduce | flops 112 | bytes 896 | tf_op jit(solution)/shard_map/psum | solution.py:80
  93.3 13.9 %all-reduce = (f32[4,4]{0,1:T(4,128)S(1)}, f32[8,4]{0,1:T(4,128)S(1)}, f32[8,8]{1,0:T(8,128)S(1)}) all-reduce(f32[4,4]{0,1:T(4,128)S(1)} %get-tuple-element.17, f32[8,4]{0,1:T(4,128)S(1)} %get-tuple-element.18, f32[8,8]{1,0:T(8,128)S(1)} %get-tuple-element.19), channel_id=1, replica_groups=mesh['clus'=8,'lvl'=4] {'clus'}, use_global_device_ids=true, to_apply=%region_9.13 | all-reduce | flops 112 | bytes 896 | tf_op jit(solution)/shard_map/psum | solution.py:79
  107.9 0.4 cholesky.55
  108.3 0.6 compare_reduce_fusion
  108.9 0.6 fusion.73
  109.6 0.3 custom-call.7
  110.2 0.6 copy.47
  110.9 0.6 pad_maximum_fusion.6
  (77 shorter events, 5.9 us)
Async XLA Ops:
  0.6 31.4 %copy-start = (bf16[1,1,4,256,256]{4,3,2,1,0:T(8,128)(2,1)S(1)}, bf16[1,1,4,256,256]{4,3,2,1,0:T(8,128)(2,1)}, u32[]{:S(2)}) copy-start(bf16[1,1,4,256,256]{4,3,2,1,0:T(8,128)(2,1)} %param.16) | copy-start | bytes 1572868
  0.6 5.2 %copy-start.4 = (f32[8,1,256]{2,1,0:T(1,128)S(1)}, f32[8,1,256]{2,1,0:T(1,128)}, u32[]{:S(2)}) copy-start(f32[8,1,256]{2,1,0:T(1,128)} %param.15) | copy-start | bytes 24580
  0.7 5.4 %copy-start.7 = (s32[1,1,4]{2,1,0:T(1,128)S(1)}, s32[1,1,4]{2,1,0:T(1,128)}, u32[]{:S(2)}) copy-start(s32[1,1,4]{2,1,0:T(1,128)} %param.17) | copy-start | bytes 52
  0.7 6.0 %copy-start.5 = (bf16[1,1,32,256]{3,2,1,0:T(8,128)(2,1)S(1)}, bf16[1,1,32,256]{3,2,1,0:T(8,128)(2,1)}, u32[]{:S(2)}) copy-start(bf16[1,1,32,256]{3,2,1,0:T(8,128)(2,1)} %param.20) | copy-start | bytes 49156
  0.7 19.7 %copy-start.8 = (s32[1,1,6]{2,1,0:T(1,128)S(1)}, s32[1,1,6]{2,1,0:T(1,128)}, u32[]{:S(2)}) copy-start(s32[1,1,6]{2,1,0:T(1,128)} %param.19) | copy-start | bytes 76
  1.4 29.3 %copy-start.1 = (f32[1,1,6,32,32]{4,3,2,1,0:T(8,128)S(1)}, f32[1,1,6,32,32]{4,3,2,1,0:T(8,128)}, u32[]{:S(2)}) copy-start(f32[1,1,6,32,32]{4,3,2,1,0:T(8,128)} %param.22) | copy-start | bytes 73732
  1.4 29.9 %collective-permute-start.1 = (bf16[4,256]{1,0:T(4,128)(2,1)S(1)}, bf16[4,256]{1,0:T(4,128)(2,1)S(1)}, u32[]{:S(2)}, u32[]{:S(2)}) collective-permute-start(bf16[4,256]{1,0:T(4,128)(2,1)S(1)} %bitcast.165), channel_id=1, source_target_pairs={{4,0},{8,4},{12,8},{16,12},{20,16},{24,20},{28,24},{5,1},{9,5},{13... | collective-permute-start | bytes 6152 | tf_op jit(solution)/shard_map/ppermute | solution.py:25
  2.9 28.5 %collective-permute-start = (bf16[4,256]{1,0:T(4,128)(2,1)S(1)}, bf16[4,256]{1,0:T(4,128)(2,1)S(1)}, u32[]{:S(2)}, u32[]{:S(2)}) collective-permute-start(bf16[4,256]{1,0:T(4,128)(2,1)S(1)} %bitcast.166), channel_id=1, source_target_pairs={{0,4},{4,8},{8,12},{12,16},{16,20},{20,24},{24,28},{1,5},{5,9},{9,... | collective-permute-start | bytes 6152 | tf_op jit(solution)/shard_map/ppermute | solution.py:22
  20.6 0.7 copy-start.3
  30.0 1.0 copy-start.2
  32.0 0.7 copy-start.6
  59.2 23.8 %collective-permute-start.3 = (bf16[4,256]{1,0:T(4,128)(2,1)S(1)}, bf16[4,256]{1,0:T(4,128)(2,1)S(1)}, u32[]{:S(2)}, u32[]{:S(2)}) collective-permute-start(bf16[4,256]{1,0:T(4,128)(2,1)S(1)} %get-tuple-element.29), channel_id=1, source_target_pairs={{4,0},{8,4},{12,8},{16,12},{20,16},{24,20},{28,24},{5,1},{9,5},{13... | collective-permute-start | bytes 6152 | tf_op jit(solution)/shard_map/ppermute | solution.py:25
  60.5 22.5 %collective-permute-start.2 = (bf16[4,256]{1,0:T(4,128)(2,1)S(1)}, bf16[4,256]{1,0:T(4,128)(2,1)S(1)}, u32[]{:S(2)}, u32[]{:S(2)}) collective-permute-start(bf16[4,256]{1,0:T(4,128)(2,1)S(1)} %get-tuple-element.29), channel_id=1, source_target_pairs={{0,4},{4,8},{8,12},{12,16},{16,20},{20,24},{24,28},{1,5},{5,9},{9,... | collective-permute-start | bytes 6152 | tf_op jit(solution)/shard_map/ppermute | solution.py:22
